TPU v7x, 32 devices: a whole 2x2x4 slice. The times are simulated.
32 devices in a mesh: gz: 2 (over y), row: 4 (over x, core), col: 4 (over z).
Axes of the slice: x: 2, y: 2, z: 4, core: 2. Of those that a mesh axis runs over, the one named last changes fastest.
Arguments:
- anc_lower: bfloat16 [1, 1024, 1024], P(None, 'col', 'row'), may hold values from -0.125 to 0.125
- anc_upper: bfloat16 [1, 1024, 1024], P(None, 'col', 'row'), may hold values from -0.125 to 0.125
- sub_lower: bfloat16 [16, 1024, 1024], P('gz', 'col', 'row'), may hold values from -0.125 to 0.125
- sub_upper: bfloat16 [16, 1024, 1024], P('gz', 'col', 'row'), may hold values from -0.125 to 0.125
- anc_rhs: bfloat16 [1, 1024, 64], P(None, 'col'), may hold values from -6 to 6
- sub_rhs: bfloat16 [6, 1024, 64], P('gz', 'col'), may hold values from -6 to 6
- layer_subtree: int32 [2], replicated, may hold values from 0 to 1, each once
- sub_pattern: int32 [10, 2], P('gz'), may hold values 0 or 1
Outputs:
- anc_solution: float32 [1, 1024, 64], P(None, ('row', 'col'))
- sub_solution: float32 [6, 1024, 64], P('gz', ('row', 'col'))
Inputs may be any that keep to these rules, and one draw needn't show every extreme that they name: `layer_subtree`: each subtree is held by exactly one layer.
All inputs are finite; a program needn't handle non-finite values. No bound on the sum of `sub_pattern` on one device may be relied on, other than what follows from the above.
Results may differ from a plain program's by a relative error of at most 0.018.
Values may be sent and summed in bfloat16 or wider, within the bound.
A program may use at most 64 MiB of HBM per device.

v0:
```python
import jax
import jax.numpy as jnp
import numpy as np
from jax import lax
from jax.sharding import PartitionSpec as P

R = 64
SUB_LEVELS = 2
SUB_NODES = 3


def level_span(depth_now):
    return (2**depth_now - 1, 2 ** (depth_now + 1) - 1)


def local_routes(first_id, stop_id, depth_now, target_count):
    table = np.zeros((target_count, (stop_id - first_id) * depth_now), np.float32)
    for offset, member in enumerate(range(first_id, stop_id)):
        for local_level in range(depth_now):
            target = (member + 1 >> depth_now - local_level) - 1
            table[target, offset * depth_now + local_level] = 1.0
    return table


def solve_diagonal(residual, blocks):
    whole_blocks = lax.all_gather(blocks, "col", axis=1, tiled=True)
    whole_res = lax.all_gather(residual, "col", axis=1, tiled=True)
    rows_full = jnp.einsum(
        "nki,nkr->nir", whole_blocks, whole_res, preferred_element_type=jnp.float32
    )
    share = rows_full.shape[1] // lax.axis_size("col")
    owned = lax.dynamic_slice_in_dim(rows_full, lax.axis_index("col") * share, share, 1)
    return (owned, rows_full.astype(jnp.bfloat16))


def upper_sum(values):
    return lax.psum(values, "row")


def local(anc_lower, anc_upper, sub_lower, sub_upper, anc_rhs, sub_rhs, layer_subtree, sub_pattern):
    layers = lax.axis_size("gz")
    levels = layers.bit_length() - 1
    anc_count = layers - 1
    row_count = lax.axis_size("row")
    col_count = lax.axis_size("col")
    rows_here = anc_lower.shape[2]
    cols_here = anc_lower.shape[1]
    sub_start = [0]
    for member in range(SUB_NODES):
        sub_start.append(sub_start[-1] + levels + (member + 1).bit_length() - 1)
    anc_start = [0]
    for member in range(anc_count):
        anc_start.append(anc_start[-1] + (member + 1).bit_length() - 1)
    low_pattern = sub_pattern[:, 0].astype(jnp.float32)
    up_pattern = sub_pattern[:, 1].astype(jnp.float32)
    layer_here = lax.axis_index("gz")
    subtree = jnp.sum(
        jnp.where(jnp.arange(layers, dtype=jnp.int32) == layer_here, layer_subtree, 0)
    )
    powers = jnp.asarray(2 ** (levels - np.arange(levels)), jnp.int32)
    heap_ids = (subtree + layers) // powers - 1
    choose = (heap_ids[:, None] == jnp.arange(anc_count, dtype=jnp.int32)[None, :]).astype(
        jnp.float32
    )
    first_layer = (layer_here == 0).astype(jnp.float32)
    row_index = lax.axis_index("row")
    col_index = lax.axis_index("col")
    holds_piece = (row_index == col_index * row_count // col_count).astype(jnp.float32)
    piece_start = jnp.clip(col_index * cols_here - row_index * rows_here, 0, rows_here - cols_here)

    def own_piece(rows_block):
        return holds_piece * lax.dynamic_slice_in_dim(rows_block, piece_start, cols_here, 1).astype(
            jnp.float32
        )

    sub_acc = jnp.zeros((SUB_NODES, cols_here, R), jnp.float32)
    to_anc = jnp.zeros((anc_count, cols_here, R), jnp.float32)
    sub_rows = {}
    for depth_now in reversed(range(SUB_LEVELS)):
        first_id, stop_id = level_span(depth_now)
        node_count = stop_id - first_id
        given = sub_rhs[first_id:stop_id].astype(jnp.float32)
        if depth_now + 1 < SUB_LEVELS:
            given = given - lax.psum(sub_acc[first_id:stop_id], "row")
        unused, solved = solve_diagonal(given.astype(jnp.bfloat16), sub_lower[first_id:stop_id])
        sub_rows[depth_now] = solved
        per_node = levels + depth_now
        opening = SUB_NODES + sub_start[first_id]
        blocks = sub_lower[opening : opening + node_count * per_node].reshape(
            node_count, per_node, cols_here, rows_here
        )
        weights = low_pattern[sub_start[first_id] : sub_start[stop_id]].reshape(
            node_count, per_node
        )
        updates = jnp.einsum("npik,nkr->npir", blocks, solved, preferred_element_type=jnp.float32)
        updates = updates * weights[:, :, None, None]
        to_anc = to_anc + jnp.einsum("ea,eir->air", choose, jnp.sum(updates[:, :levels], 0))
        if depth_now > 0:
            table = jnp.asarray(local_routes(first_id, stop_id, depth_now, SUB_NODES))
            sub_acc = sub_acc + jnp.einsum(
                "tq,qir->tir", table, updates[:, levels:].reshape(-1, cols_here, R)
            )
    anc_acc = jnp.zeros((anc_count, cols_here, R), jnp.float32)
    anc_rows = {}
    for depth_now in reversed(range(levels)):
        first_id, stop_id = level_span(depth_now)
        node_count = stop_id - first_id
        joined = to_anc[first_id:stop_id] + first_layer * anc_acc[first_id:stop_id]
        reached = lax.psum(joined, ("gz", "row"))
        given = anc_rhs[first_id:stop_id].astype(jnp.float32) - reached
        unused, solved = solve_diagonal(given.astype(jnp.bfloat16), anc_lower[first_id:stop_id])
        anc_rows[depth_now] = solved
        if depth_now > 0:
            opening = anc_count + anc_start[first_id]
            blocks = anc_lower[opening : opening + node_count * depth_now].reshape(
                node_count, depth_now, cols_here, rows_here
            )
            updates = jnp.einsum(
                "npik,nkr->npir", blocks, solved, preferred_element_type=jnp.float32
            )
            table = jnp.asarray(local_routes(first_id, stop_id, depth_now, anc_count))
            anc_acc = anc_acc + jnp.einsum("tq,qir->tir", table, updates.reshape(-1, cols_here, R))
    anc_z_parts = []
    anc_out_parts = []
    for depth_now in range(levels):
        first_id, stop_id = level_span(depth_now)
        node_count = stop_id - first_id
        given = own_piece(anc_rows[depth_now])
        if depth_now > 0:
            z_sofar = jnp.concatenate(anc_z_parts, 0)
            table = local_routes(first_id, stop_id, depth_now, anc_count)[:first_id].T
            sources = jnp.einsum(
                "qa,akr->qkr",
                jnp.asarray(table, jnp.bfloat16),
                z_sofar,
                preferred_element_type=jnp.float32,
            )
            sources = sources.astype(jnp.bfloat16).reshape(node_count, depth_now, rows_here, R)
            opening = anc_count + anc_start[first_id]
            blocks = anc_upper[opening : opening + node_count * depth_now].reshape(
                node_count, depth_now, cols_here, rows_here
            )
            updates = jnp.einsum(
                "npik,npkr->npir", blocks, sources, preferred_element_type=jnp.float32
            )
            given = given - jnp.sum(updates, 1)
        summed = upper_sum(given)
        owned, solved = solve_diagonal(summed.astype(jnp.bfloat16), anc_upper[first_id:stop_id])
        anc_out_parts.append(owned)
        anc_z_parts.append(solved)
    anc_z_all = jnp.concatenate(anc_z_parts, 0)
    selected = jnp.einsum(
        "ea,akr->ekr", choose.astype(jnp.bfloat16), anc_z_all, preferred_element_type=jnp.float32
    )
    selected = selected.astype(jnp.bfloat16)
    sub_z_parts = []
    sub_out_parts = []
    for depth_now in range(SUB_LEVELS):
        first_id, stop_id = level_span(depth_now)
        node_count = stop_id - first_id
        per_node = levels + depth_now
        opening = SUB_NODES + sub_start[first_id]
        blocks = sub_upper[opening : opening + node_count * per_node].reshape(
            node_count, per_node, cols_here, rows_here
        )
        weights = up_pattern[sub_start[first_id] : sub_start[stop_id]].reshape(node_count, per_node)
        updates = jnp.einsum(
            "npik,pkr->npir", blocks[:, :levels], selected, preferred_element_type=jnp.float32
        )
        if depth_now > 0:
            z_sofar = sub_z_parts[0]
            table = local_routes(first_id, stop_id, depth_now, SUB_NODES)[:first_id].T
            sources = jnp.einsum(
                "qa,akr->qkr",
                jnp.asarray(table, jnp.bfloat16),
                z_sofar,
                preferred_element_type=jnp.float32,
            )
            sources = sources.astype(jnp.bfloat16).reshape(node_count, depth_now, rows_here, R)
            local_updates = jnp.einsum(
                "npik,npkr->npir", blocks[:, levels:], sources, preferred_element_type=jnp.float32
            )
            updates = jnp.concatenate([updates, local_updates], 1)
        change = jnp.sum(updates * weights[:, :, None, None], 1)
        summed = upper_sum(own_piece(sub_rows[depth_now]) - change)
        owned, solved = solve_diagonal(summed.astype(jnp.bfloat16), sub_upper[first_id:stop_id])
        sub_out_parts.append(owned)
        sub_z_parts.append(solved)
    return (jnp.concatenate(anc_out_parts, 0), jnp.concatenate(sub_out_parts, 0))


def solution(mesh):
    in_specs = (
        P(None, "col", "row"),
        P(None, "col", "row"),
        P("gz", "col", "row"),
        P("gz", "col", "row"),
        P(None, "col", None),
        P("gz", "col", None),
        P(),
        P("gz", None),
    )
    out_specs = (P(None, ("row", "col"), None), P("gz", ("row", "col"), None))
    return jax.shard_map(local, mesh=mesh, in_specs=in_specs, out_specs=out_specs, check_vma=False)
```

profile of v0, /device:TPU:0, one launch (start us, length us, event | category | flops | bytes accessed | tf_op | source)
XLA Modules:
  0.0 251.9 jit_solution(8480645708661849595)
XLA Ops:
  7.2 1.7 slice.67
  9.0 0.6 copy-done.7
  9.6 0.6 fusion.35
  11.0 0.7 copy-done.6
  11.8 17.3 %all_gather.37 = bf16[2,1024,64]{1,2,0:T(8,128)(2,1)S(1)} all-gather(bf16[2,256,64]{1,2,0:T(8,128)(2,1)S(1)} %slice-done.3), channel_id=1, replica_groups=mesh['gz'=2,'row'=4,'col'=4] {'col'}, dimensions={1}, use_global_device_ids=true | all-gather | bytes 327680 | tf_op jit(solution)/shard_map/all_gather | solution.py:27
  29.1 22.6 %all_gather.39 = bf16[1,1024,256]{2,1,0:T(8,128)(2,1)S(1)} all-gather(bf16[1,256,256]{2,1,0:T(8,128)(2,1)S(1)} %slice-done.1), channel_id=1, replica_groups=mesh['gz'=2,'row'=4,'col'=4] {'col'}, dimensions={1}, use_global_device_ids=true | all-gather | bytes 655360 | tf_op jit(solution)/shard_map/all_gather | solution.py:26
  51.7 1.6 convolution_convert_fusion
  53.4 0.3 fusion
  53.7 0.3 copy-done.8
  54.0 0.9 fusion.27
  55.0 30.0 %all-reduce.4.cloned.1.call-done = f32[1,256,64]{1,0,2:T(1,128)} async-done(((f32[1,256,64]{1,0,2:T(1,128)}), f32[1,256,64]{1,0,2:T(1,128)}) %all-reduce.4.cloned.1.call-update) | async-done | bytes 65552 | tf_op jit(solution)/shard_map/psum | solution.py:84
  85.0 0.9 fusion.30
  85.9 13.5 %all_gather.38 = bf16[1,1024,64]{1,0,2:T(2,128)(2,1)S(1)} all-gather(bf16[1,256,64]{1,0,2:T(2,128)(2,1)S(1)} %fusion.30), channel_id=1, replica_groups=mesh['gz'=2,'row'=4,'col'=4] {'col'}, dimensions={1}, use_global_device_ids=true | all-gather | bytes 163840 | tf_op jit(solution)/shard_map/all_gather | solution.py:27
  99.4 0.2 convolution_convert_fusion.2
  99.6 0.9 fusion.7
  100.5 0.7 slice.87
  101.4 0.8 copy-done.3
  102.2 14.9 %all_gather.41 = bf16[1,1024,256]{2,1,0:T(8,128)(2,1)S(1)} all-gather(bf16[1,256,256]{2,1,0:T(8,128)(2,1)S(1)} %copy-done.3), channel_id=1, replica_groups=mesh['gz'=2,'row'=4,'col'=4] {'col'}, dimensions={1}, use_global_device_ids=true | all-gather | bytes 655360 | tf_op jit(solution)/shard_map/all_gather | solution.py:26
  117.1 16.3 %all_gather.43 = bf16[1,1024,256]{2,1,0:T(8,128)(2,1)S(1)} all-gather(bf16[1,256,256]{2,1,0:T(8,128)(2,1)S(1)} %copy-done.4), channel_id=1, replica_groups=mesh['gz'=2,'row'=4,'col'=4] {'col'}, dimensions={1}, use_global_device_ids=true | all-gather | bytes 655360 | tf_op jit(solution)/shard_map/all_gather | solution.py:26
  133.4 14.8 %all_gather.45 = bf16[1,1024,256]{2,1,0:T(8,128)(2,1)S(1)} all-gather(bf16[1,256,256]{2,1,0:T(8,128)(2,1)S(1)} %slice-done.2), channel_id=1, replica_groups=mesh['gz'=2,'row'=4,'col'=4] {'col'}, dimensions={1}, use_global_device_ids=true | all-gather | bytes 655360 | tf_op jit(solution)/shard_map/all_gather | solution.py:26
  148.5 2.8 %all-reduce.6.cloned.1.call-done = f32[1,256,64]{1,2,0:T(8,128)} async-done(((f32[1,256,64]{1,2,0:T(8,128)}), f32[1,256,64]{1,2,0:T(8,128)}) %all-reduce.6.cloned.1.call-update) | async-done | bytes 65552 | tf_op jit(solution)/shard_map/psum | solution.py:109
  151.3 0.8 subtract_convert_fusion
  152.1 13.9 %all_gather.40 = bf16[1,1024,64]{1,2,0:T(8,128)(2,1)S(1)} all-gather(bf16[1,256,64]{1,2,0:T(8,128)(2,1)S(1)} %subtract_convert_fusion), channel_id=1, replica_groups=mesh['gz'=2,'row'=4,'col'=4] {'col'}, dimensions={1}, use_global_device_ids=true | all-gather | bytes 163840 | tf_op jit(solution)/shard_map/all_gather | solution.py:27
  166.2 11.5 %psum.37 = bf16[1,256,64]{1,2,0:T(8,128)(2,1)S(1)} all-reduce(f32[1,256,64]{1,2,0:T(8,128)S(1)} %fusion.10), channel_id=1, replica_groups=mesh['gz'=2,'row'=4,'col'=4] {'row'}, use_global_device_ids=true, to_apply=%region_4.5 | all-reduce | flops 16384 | bytes 98304 | tf_op jit(solution)/shard_map/psum | solution.py:37
  177.7 13.4 %all_gather.42 = bf16[1,1024,64]{1,2,0:T(8,128)(2,1)S(1)} all-gather(bf16[1,256,64]{1,2,0:T(8,128)(2,1)S(1)} %psum.37), channel_id=1, replica_groups=mesh['gz'=2,'row'=4,'col'=4] {'col'}, dimensions={1}, use_global_device_ids=true | all-gather | bytes 163840 | tf_op jit(solution)/shard_map/all_gather | solution.py:27
  191.5 10.7 %psum.38 = bf16[1,256,64]{1,2,0:T(8,128)(2,1)S(1)} all-reduce(f32[1,256,64]{1,2,0:T(8,128)S(1)} %fusion.3), channel_id=1, replica_groups=mesh['gz'=2,'row'=4,'col'=4] {'row'}, use_global_device_ids=true, to_apply=%region_5.6 | all-reduce | flops 16384 | bytes 98304 | tf_op jit(solution)/shard_map/psum | solution.py:37
  202.2 13.3 %all_gather.44 = bf16[1,1024,64]{1,2,0:T(8,128)(2,1)S(1)} all-gather(bf16[1,256,64]{1,2,0:T(8,128)(2,1)S(1)} %psum.38), channel_id=1, replica_groups=mesh['gz'=2,'row'=4,'col'=4] {'col'}, dimensions={1}, use_global_device_ids=true | all-gather | bytes 163840 | tf_op jit(solution)/shard_map/all_gather | solution.py:27
  216.3 11.9 %all-reduce.7 = bf16[2,256,64]{1,2,0:T(8,128)(2,1)S(1)} all-reduce(f32[2,256,64]{1,2,0:T(8,128)S(1)} %multiply_subtract_fusion), channel_id=1, replica_groups=mesh['gz'=2,'row'=4,'col'=4] {'row'}, use_global_device_ids=true, to_apply=%region_7.8 | all-reduce | flops 32768 | bytes 196608 | tf_op jit(solution)/shard_map/psum | solution.py:37
  228.2 14.0 %all_gather.46 = bf16[2,1024,64]{1,2,0:T(8,128)(2,1)S(1)} all-gather(bf16[2,256,64]{1,2,0:T(8,128)(2,1)S(1)} %all-reduce.7), channel_id=1, replica_groups=mesh['gz'=2,'row'=4,'col'=4] {'col'}, dimensions={1}, use_global_device_ids=true | all-gather | bytes 327680 | tf_op jit(solution)/shard_map/all_gather | solution.py:27
  242.3 1.5 fusion.36
  243.9 0.7 copy.24
  244.7 0.7 copy.23
  (56 shorter events, 2.4 us)
Async XLA Ops:
  7.2 44.6 %all-gather.3.cloned.1.call-start = ((), (), s32[]{:S(2)}) async-start(), calls=%async_computation | async-start | bytes 1310720 | tf_op jit(solution)/shard_map/all_gather | solution.py:26
  8.9 76.1 %all-reduce.4.cloned.1.call-start = ((), (), s32[]{:S(2)}) async-start(), calls=%async_computation.1 | async-start | bytes 131072 | tf_op jit(solution)/shard_map/psum | solution.py:84
  9.0 0.7 copy-start.7
  10.9 0.9 slice-start.3
  10.9 0.7 copy-start.6
  11.8 17.3 %slice-start.1 = ((bf16[8,256,256]{2,1,0:T(8,128)(2,1)}), bf16[1,256,256]{2,1,0:T(8,128)(2,1)S(1)}, s32[]{:S(2)}) async-start(bf16[8,256,256]{2,1,0:T(8,128)(2,1)} %param.13), calls=%async_computation.5 | async-start | bytes 262144 | tf_op jit(solution)/shard_map/slice | solution.py:85
  51.7 1.6 slice-start
  53.3 0.7 copy-start.8
  53.3 31.7 %slice-start.4 = ((bf16[3,256,64]{1,2,0:T(8,128)(2,1)}), bf16[1,256,64]{1,2,0:T(8,128)(2,1)S(1)}, s32[]{:S(2)}) async-start(bf16[3,256,64]{1,2,0:T(8,128)(2,1)} %param.16), calls=%async_computation.8 | async-start | bytes 65536 | tf_op jit(solution)/shard_map/slice | solution.py:82
  53.6 46.0 %copy-start = (bf16[8,256,256]{2,1,0:T(8,128)(2,1)S(1)}, bf16[8,256,256]{2,1,0:T(8,128)(2,1)}, u32[]{:S(2)}) copy-start(bf16[8,256,256]{2,1,0:T(8,128)(2,1)} %param.13) | copy-start | bytes 3145732
  54.0 46.5 %copy-start.1 = (bf16[8,256,256]{2,1,0:T(8,128)(2,1)S(1)}, bf16[8,256,256]{2,1,0:T(8,128)(2,1)}, u32[]{:S(2)}) copy-start(bf16[8,256,256]{2,1,0:T(8,128)(2,1)} %param.14) | copy-start | bytes 3145732
  54.9 96.3 %all-reduce.6.cloned.1.call-start = ((), (), s32[]{:S(2)}) async-start(), calls=%async_computation.2 | async-start | bytes 131072 | tf_op jit(solution)/shard_map/psum | solution.py:109
  100.5 141.8 %all-gather.5.cloned.1.call-start = ((), (), s32[]{:S(2)}) async-start(), calls=%async_computation.3 | async-start | bytes 1310720 | tf_op jit(solution)/shard_map/all_gather | solution.py:26
  101.3 0.9 copy-start.3
  102.2 14.9 %copy-start.4 = (bf16[1,256,256]{2,1,0:T(8,128)(2,1)S(1)}, bf16[1,256,256]{2,1,0:T(8,128)(2,1)}, u32[]{:S(2)}) copy-start(bf16[1,256,256]{2,1,0:T(8,128)(2,1)} %param.12) | copy-start | bytes 393220
  117.1 16.3 %slice-start.2 = ((bf16[8,256,256]{2,1,0:T(8,128)(2,1)}), bf16[1,256,256]{2,1,0:T(8,128)(2,1)S(1)}, s32[]{:S(2)}) async-start(bf16[8,256,256]{2,1,0:T(8,128)(2,1)} %param.14), calls=%async_computation.6 | async-start | bytes 262144 | tf_op jit(solution)/shard_map/slice | solution.py:186
  133.4 17.9 %copy-start.5 = (bf16[1,256,64]{1,2,0:T(8,128)(2,1)S(1)}, bf16[1,256,64]{1,2,0:T(8,128)(2,1)}, u32[]{:S(2)}) copy-start(bf16[1,256,64]{1,2,0:T(8,128)(2,1)} %param.15) | copy-start | bytes 98308
  148.2 43.1 %copy-start.2 = (bf16[8,256,256]{2,1,0:T(8,128)(2,1)S(1)}, bf16[8,256,256]{2,1,0:T(8,128)(2,1)}, u32[]{:S(2)}) copy-start(bf16[8,256,256]{2,1,0:T(8,128)(2,1)} %param.14) | copy-start | bytes 3145732
Sparse Core Ops, SparseCore 0:
  9.5 40.4 all-gather.2
  55.0 29.9 all-reduce.3
  100.6 50.5 all-reduce.5
  152.7 27.7 all-gather.4
where the time goes:
time: 253 us; the launch traced here: 252 us
  blocking collectives  188 us (74%)
  waiting for transfers between devices  32.9 us (13%)
  between operations  14.7 us (6%)
  local copies, waits for them, and re-layouts  7.11 us (3%)
  matrix products  6.59 us (3%)
    all_gather x6, blocking collectives, solve_diagonal(): whole_res = lax.all_gather(residual, 'col', axis=1, tiled=True)  85.3 us
    all_gather x4, blocking collectives, solve_diagonal(): whole_blocks = lax.all_gather(blocks, 'col', axis=1, tiled=True)  68.6 us
    psum x3, blocking collectives, upper_sum(): return lax.psum(values, 'row')  34 us
    psum x1, waiting for transfers between devices, local(): given = given - lax.psum(sub_acc[first_id:stop_id], 'row')  30 us
  transfers between devices with their start and end apart: 4, of which 2 were waited for; matrix products, arithmetic and copies ran while one was open for 2% of the time, Pallas kernels for 0%

commit v1 on v0

--- a/solution.py
+++ b/solution.py
@@ -81,7 +81,7 @@
         node_count = stop_id - first_id
         given = sub_rhs[first_id:stop_id].astype(jnp.float32)
         if depth_now + 1 < SUB_LEVELS:
-            given = given - lax.psum(sub_acc[first_id:stop_id], "row")
+            given = given - jnp.sum(lax.all_gather(sub_acc[first_id:stop_id], "row"), axis=0)
         unused, solved = solve_diagonal(given.astype(jnp.bfloat16), sub_lower[first_id:stop_id])
         sub_rows[depth_now] = solved
         per_node = levels + depth_now

time: 253 us -> 229 us (0.905)
  waiting for transfers between devices: 32.9 us -> 3.96 us
  blocking collectives: 188 us -> 194 us
    psum x1 -> x0, waiting for transfers between devices: 30 us -> none  [local(): given = given - lax.psum(sub_acc[first_id:stop_id], 'row')]
    all_gather x0 -> x1, blocking collectives: none -> 5.91 us  [local(): lax.all_gather(sub_acc[first_id:stop_id], 'row')]
  transfers between devices with their start and end apart: 4 -> 3, of which waited for: 2 -> 1; matrix products, arithmetic and copies ran while one was open for 2% -> 2% of each run, Pallas kernels for 0% -> 0%
where the time goes in v1:
time: 229 us
  blocking collectives  194 us (85%)
  between operations  14.7 us (6%)
  local copies, waits for them, and re-layouts  8.24 us (4%)
  matrix products  5.93 us (3%)
  waiting for transfers between devices  3.96 us (2%)
    all_gather x6, blocking collectives, solve_diagonal(): whole_res = lax.all_gather(residual, 'col', axis=1, tiled=True)  85.7 us
    all_gather x4, blocking collectives, solve_diagonal(): whole_blocks = lax.all_gather(blocks, 'col', axis=1, tiled=True)  68.5 us
    psum x3, blocking collectives, upper_sum(): return lax.psum(values, 'row')  34 us
    all_gather x1, blocking collectives, local(): lax.all_gather(sub_acc[first_id:stop_id], 'row')  5.91 us
  transfers between devices with their start and end apart: 3, of which 1 were waited for; matrix products, arithmetic and copies ran while one was open for 2% of the time, Pallas kernels for 0%

profile of v1, /device:TPU:0, one launch (start us, length us, event | category | flops | bytes accessed | tf_op | source)
XLA Modules:
  0.0 228.7 jit_solution(2245774289420561933)
XLA Ops:
  7.2 1.7 slice.67
  9.0 0.6 copy-done.8
  9.6 0.6 fusion.33
  11.0 0.7 copy-done.7
  11.8 0.8 slice-done.3
  12.6 17.5 %all_gather.43 = bf16[2,1024,64]{1,2,0:T(8,128)(2,1)S(1)} all-gather(bf16[2,256,64]{1,2,0:T(8,128)(2,1)S(1)} %slice-done.3), channel_id=1, replica_groups=mesh['gz'=2,'row'=4,'col'=4] {'col'}, dimensions={1}, use_global_device_ids=true | all-gather | bytes 327680 | tf_op jit(solution)/shard_map/all_gather | solution.py:27
  30.1 22.7 %all_gather.47 = bf16[1,1024,256]{2,1,0:T(8,128)(2,1)S(1)} all-gather(bf16[1,256,256]{2,1,0:T(8,128)(2,1)S(1)} %slice-done.1), channel_id=1, replica_groups=mesh['gz'=2,'row'=4,'col'=4] {'col'}, dimensions={1}, use_global_device_ids=true | all-gather | bytes 655360 | tf_op jit(solution)/shard_map/all_gather | solution.py:26
  52.9 1.6 convolution_convert_fusion
  54.5 0.3 fusion
  54.8 0.6 copy-done.9
  55.4 0.3 fusion.26
  55.7 5.9 %all-gather = f32[4,256,64]{1,2,0:T(8,128)S(1)} all-gather(f32[1,256,64]{1,2,0:T(8,128)S(1)} %copy.24), channel_id=2, replica_groups=mesh['gz'=2,'row'=4,'col'=4] {'row'}, dimensions={0}, use_global_device_ids=true | all-gather | bytes 327680 | tf_op jit(solution)/shard_map/all_gather | solution.py:84
  61.7 13.7 %all_gather.46 = bf16[1,1024,64]{1,2,0:T(8,128)(2,1)S(1)} all-gather(bf16[1,256,64]{1,2,0:T(8,128)(2,1)S(1)} %fusion.29), channel_id=1, replica_groups=mesh['gz'=2,'row'=4,'col'=4] {'col'}, dimensions={1}, use_global_device_ids=true | all-gather | bytes 163840 | tf_op jit(solution)/shard_map/all_gather | solution.py:27
  75.3 0.2 convolution_convert_fusion.2
  75.5 0.9 fusion.7
  76.5 0.7 slice.87
  77.3 0.8 copy-done.4
  78.2 15.0 %all_gather.49 = bf16[1,1024,256]{2,1,0:T(8,128)(2,1)S(1)} all-gather(bf16[1,256,256]{2,1,0:T(8,128)(2,1)S(1)} %copy-done.4), channel_id=1, replica_groups=mesh['gz'=2,'row'=4,'col'=4] {'col'}, dimensions={1}, use_global_device_ids=true | all-gather | bytes 655360 | tf_op jit(solution)/shard_map/all_gather | solution.py:26
  93.2 15.8 %all_gather.51 = bf16[1,1024,256]{2,1,0:T(8,128)(2,1)S(1)} all-gather(bf16[1,256,256]{2,1,0:T(8,128)(2,1)S(1)} %copy-done.5), channel_id=1, replica_groups=mesh['gz'=2,'row'=4,'col'=4] {'col'}, dimensions={1}, use_global_device_ids=true | all-gather | bytes 655360 | tf_op jit(solution)/shard_map/all_gather | solution.py:26
  108.9 15.0 %all_gather.53 = bf16[1,1024,256]{2,1,0:T(8,128)(2,1)S(1)} all-gather(bf16[1,256,256]{2,1,0:T(8,128)(2,1)S(1)} %slice-done.2), channel_id=1, replica_groups=mesh['gz'=2,'row'=4,'col'=4] {'col'}, dimensions={1}, use_global_device_ids=true | all-gather | bytes 655360 | tf_op jit(solution)/shard_map/all_gather | solution.py:26
  124.2 3.9 %all-reduce.3.cloned.1.call-done = f32[1,256,64]{1,2,0:T(8,128)} async-done(((f32[1,256,64]{1,2,0:T(8,128)}), f32[1,256,64]{1,2,0:T(8,128)}) %all-reduce.3.cloned.1.call-update) | async-done | bytes 65552 | tf_op jit(solution)/shard_map/psum | solution.py:109
  128.1 0.8 subtract_convert_fusion
  129.0 13.9 %all_gather.48 = bf16[1,1024,64]{1,2,0:T(8,128)(2,1)S(1)} all-gather(bf16[1,256,64]{1,2,0:T(8,128)(2,1)S(1)} %subtract_convert_fusion), channel_id=1, replica_groups=mesh['gz'=2,'row'=4,'col'=4] {'col'}, dimensions={1}, use_global_device_ids=true | all-gather | bytes 163840 | tf_op jit(solution)/shard_map/all_gather | solution.py:27
  143.0 11.5 %psum.29 = bf16[1,256,64]{1,2,0:T(8,128)(2,1)S(1)} all-reduce(f32[1,256,64]{1,2,0:T(8,128)S(1)} %fusion.10), channel_id=1, replica_groups=mesh['gz'=2,'row'=4,'col'=4] {'row'}, use_global_device_ids=true, to_apply=%region_4.5 | all-reduce | flops 16384 | bytes 98304 | tf_op jit(solution)/shard_map/psum | solution.py:37
  154.5 13.4 %all_gather.50 = bf16[1,1024,64]{1,2,0:T(8,128)(2,1)S(1)} all-gather(bf16[1,256,64]{1,2,0:T(8,128)(2,1)S(1)} %psum.29), channel_id=1, replica_groups=mesh['gz'=2,'row'=4,'col'=4] {'col'}, dimensions={1}, use_global_device_ids=true | all-gather | bytes 163840 | tf_op jit(solution)/shard_map/all_gather | solution.py:27
  168.3 10.7 %psum.30 = bf16[1,256,64]{1,2,0:T(8,128)(2,1)S(1)} all-reduce(f32[1,256,64]{1,2,0:T(8,128)S(1)} %fusion.3), channel_id=1, replica_groups=mesh['gz'=2,'row'=4,'col'=4] {'row'}, use_global_device_ids=true, to_apply=%region_5.6 | all-reduce | flops 16384 | bytes 98304 | tf_op jit(solution)/shard_map/psum | solution.py:37
  179.0 13.4 %all_gather.52 = bf16[1,1024,64]{1,2,0:T(8,128)(2,1)S(1)} all-gather(bf16[1,256,64]{1,2,0:T(8,128)(2,1)S(1)} %psum.30), channel_id=1, replica_groups=mesh['gz'=2,'row'=4,'col'=4] {'col'}, dimensions={1}, use_global_device_ids=true | all-gather | bytes 163840 | tf_op jit(solution)/shard_map/all_gather | solution.py:27
  193.1 11.9 %all-reduce.4 = bf16[2,256,64]{1,2,0:T(8,128)(2,1)S(1)} all-reduce(f32[2,256,64]{1,2,0:T(8,128)S(1)} %multiply_subtract_fusion), channel_id=1, replica_groups=mesh['gz'=2,'row'=4,'col'=4] {'row'}, use_global_device_ids=true, to_apply=%region_7.8 | all-reduce | flops 32768 | bytes 196608 | tf_op jit(solution)/shard_map/psum | solution.py:37
  205.0 14.0 %all_gather.54 = bf16[2,1024,64]{1,2,0:T(8,128)(2,1)S(1)} all-gather(bf16[2,256,64]{1,2,0:T(8,128)(2,1)S(1)} %all-reduce.4), channel_id=1, replica_groups=mesh['gz'=2,'row'=4,'col'=4] {'col'}, dimensions={1}, use_global_device_ids=true | all-gather | bytes 327680 | tf_op jit(solution)/shard_map/all_gather | solution.py:27
  219.1 1.5 fusion.34
  220.7 0.7 copy.29
  221.5 0.7 copy.28
  (56 shorter events, 2.3 us)
Async XLA Ops:
  7.2 45.7 %all-gather.4.cloned.1.call-start = ((), (), s32[]{:S(2)}) async-start(), calls=%async_computation | async-start | bytes 1310720 | tf_op jit(solution)/shard_map/all_gather | solution.py:26
  8.9 119.2 %all-reduce.3.cloned.1.call-start = ((), (), s32[]{:S(2)}) async-start(), calls=%async_computation.1 | async-start | bytes 131072 | tf_op jit(solution)/shard_map/psum | solution.py:109
  9.0 0.7 copy-start.8
  10.9 0.7 copy-start.7
  11.8 0.8 slice-start.3
  12.6 17.5 %slice-start.1 = ((bf16[8,256,256]{2,1,0:T(8,128)(2,1)}), bf16[1,256,256]{2,1,0:T(8,128)(2,1)S(1)}, s32[]{:S(2)}) async-start(bf16[8,256,256]{2,1,0:T(8,128)(2,1)} %param.13), calls=%async_computation.4 | async-start | bytes 262144 | tf_op jit(solution)/shard_map/slice | solution.py:85
  52.9 1.6 slice-start
  54.8 0.7 copy-start.9
  54.8 6.9 %copy-start.3 = (bf16[3,256,64]{1,2,0:T(8,128)(2,1)S(1)}, bf16[3,256,64]{1,2,0:T(8,128)(2,1)}, u32[]{:S(2)}) copy-start(bf16[3,256,64]{1,2,0:T(8,128)(2,1)} %param.16) | copy-start | bytes 294916
  55.4 20.1 %copy-start = (bf16[8,256,256]{2,1,0:T(8,128)(2,1)S(1)}, bf16[8,256,256]{2,1,0:T(8,128)(2,1)}, u32[]{:S(2)}) copy-start(bf16[8,256,256]{2,1,0:T(8,128)(2,1)} %param.13) | copy-start | bytes 3145732
  55.7 20.8 %copy-start.1 = (bf16[8,256,256]{2,1,0:T(8,128)(2,1)S(1)}, bf16[8,256,256]{2,1,0:T(8,128)(2,1)}, u32[]{:S(2)}) copy-start(bf16[8,256,256]{2,1,0:T(8,128)(2,1)} %param.14) | copy-start | bytes 3145732
  76.4 142.7 %all-gather.6.cloned.1.call-start = ((), (), s32[]{:S(2)}) async-start(), calls=%async_computation.2 | async-start | bytes 1310720 | tf_op jit(solution)/shard_map/all_gather | solution.py:26
  77.3 0.9 copy-start.4
  78.2 15.0 %copy-start.5 = (bf16[1,256,256]{2,1,0:T(8,128)(2,1)S(1)}, bf16[1,256,256]{2,1,0:T(8,128)(2,1)}, u32[]{:S(2)}) copy-start(bf16[1,256,256]{2,1,0:T(8,128)(2,1)} %param.12) | copy-start | bytes 393220
  93.2 15.8 %slice-start.2 = ((bf16[8,256,256]{2,1,0:T(8,128)(2,1)}), bf16[1,256,256]{2,1,0:T(8,128)(2,1)S(1)}, s32[]{:S(2)}) async-start(bf16[8,256,256]{2,1,0:T(8,128)(2,1)} %param.14), calls=%async_computation.5 | async-start | bytes 262144 | tf_op jit(solution)/shard_map/slice | solution.py:186
  108.9 19.2 %copy-start.6 = (bf16[1,256,64]{1,2,0:T(8,128)(2,1)S(1)}, bf16[1,256,64]{1,2,0:T(8,128)(2,1)}, u32[]{:S(2)}) copy-start(bf16[1,256,64]{1,2,0:T(8,128)(2,1)} %param.15) | copy-start | bytes 98308
  123.9 44.1 %copy-start.2 = (bf16[8,256,256]{2,1,0:T(8,128)(2,1)S(1)}, bf16[8,256,256]{2,1,0:T(8,128)(2,1)}, u32[]{:S(2)}) copy-start(bf16[8,256,256]{2,1,0:T(8,128)(2,1)} %param.14) | copy-start | bytes 3145732
Sparse Core Ops, SparseCore 0:
  9.5 40.6 all-gather.3
  76.5 51.5 all-reduce.2
  129.7 27.7 all-gather.5
